TPU v7x, 32 devices: a whole 2x2x4 slice. The times are simulated.
32 devices in a mesh: region: 1, band: 32 (over z, y, x, core), tile: 1, sub: 1.
Axes of the slice: x: 2, y: 2, z: 4, core: 2. Of those that a mesh axis runs over, the one named last changes fastest.
Arguments:
- scenes: bfloat16 [60, 6, 1024, 128], P(('region', 'tile'), 'sub', 'band'), may hold values from -6 to 6
- clear_bits: int32 [2, 32, 256], P(('region', 'tile'), 'band'), may hold values from 0 to 1073741823
- footprint: int32 [60, 2], P(('region', 'tile')), may hold values from 0 to 31, as said below
- offsets: int32 [60, 2], P(('region', 'tile')), may hold values from 0 to 15
- acq_day: int32 [60], P(('region', 'tile')), may hold values from 0 to 364
Outputs:
- coefficients: float32 [8, 6, 128, 1024], P('region', 'sub', 'band', 'tile')
- monthly: float32 [12, 6, 128, 1024], P(('region', 'tile'), 'sub', 'band')
- annual: float32 [6, 128, 1024], P(('region', 'sub'), 'band', 'tile')
Inputs may be any that keep to these rules, and one draw needn't show every extreme that they name: `clear_bits`: bit j (j < 30) of word w at cell (b, a) is 1 when date 30 w + j is clear over columns 4 b to 4 b + 3 and rows 4 a to 4 a + 3. footprint[t, 0] <= footprint[t, 1]; date t's scene covers columns 4 * footprint[t, 0] to 4 * (footprint[t, 1] + 1) - 1. `offsets`: offsets in sixteenths of a pixel, along rows then columns.
All inputs are finite; a program needn't handle non-finite values.
Results may differ from a plain program's by a relative error of at most 0.005.
Values may be sent and summed in bfloat16 or wider, within the bound.
A program may use at most 64 MiB of HBM per device.

v0:
```python
import functools

import jax
import jax.numpy as jnp
from jax import lax
from jax.experimental import pallas as pl
from jax.experimental.pallas import tpu as pltpu
from jax.sharding import PartitionSpec as P

RIDGE = 1.0


def shifted(value, axis, steps):
    count = lax.axis_size(axis)
    first, last = (max(0, -steps), min(count, count - steps))
    return lax.ppermute(value, axis, [(source, source + steps) for source in range(first, last)])


def extended(x, sides, width):
    for axis, dim in sides:
        devices, length = (lax.axis_size(axis), x.shape[dim])
        up = [(i, (i + 1) % devices) for i in range(devices - 1)]
        down = [(j, i) for i, j in up]
        last = lax.slice_in_dim(x, length - width, length, axis=dim)
        first = lax.slice_in_dim(x, 0, width, axis=dim)
        before = lax.ppermute(last, axis, up)
        after = lax.ppermute(first, axis, down)
        x = jnp.concatenate([before, x, after], axis=dim)
    return x


def design_tables(acq_day):
    day_phase = acq_day.astype(jnp.float32) / 365.0
    columns = [jnp.ones_like(day_phase), 2.0 * day_phase - 1.0]
    for harmonic in (1, 2, 3):
        turn_angle = 2.0 * jnp.pi * harmonic * day_phase
        columns = columns + [jnp.cos(turn_angle), jnp.sin(turn_angle)]
    harmonic_basis = jnp.stack(columns, axis=1)
    month_index = acq_day * 12 // 365
    onehot = (month_index[:, None] == jnp.arange(12, dtype=jnp.int32)[None, :]).astype(jnp.float32)
    products = jnp.stack(
        [
            harmonic_basis[:, row_term] * harmonic_basis[:, col_term]
            for row_term in range(8)
            for col_term in range(row_term + 1)
        ],
        axis=1,
    )
    return (
        jnp.concatenate([products, onehot], axis=1),
        jnp.concatenate([harmonic_basis, onehot], axis=1),
    )


def bilinear(padded, offsets):
    shift_row = (offsets[:, 0].astype(jnp.float32) / 16.0)[:, None, None, None]
    shift_col = (offsets[:, 1].astype(jnp.float32) / 16.0)[:, None, None, None]
    upper_rows = padded[:, :, :-1].astype(jnp.float32)
    lower_rows = padded[:, :, 1:].astype(jnp.float32)

    def across(source):
        right_cell = jnp.concatenate([source[..., 1:], jnp.zeros_like(source[..., :1])], axis=-1)
        return (1.0 - shift_col) * source + shift_col * right_cell

    return ((1.0 - shift_row) * across(upper_rows) + shift_row * across(lower_rows)).astype(
        jnp.bfloat16
    )


def clear_weight(cell_words, footprint, strip_width):
    date_count = footprint.shape[0]
    per_date = jnp.repeat(cell_words, 30, axis=0)
    bit_place = (jnp.arange(date_count, dtype=jnp.int32) % 30)[:, None, None]
    clear_flag = jnp.right_shift(per_date, bit_place) & 1
    pixel_flag = jnp.repeat(jnp.repeat(clear_flag, 4, axis=1), 4, axis=2)
    strip_index = jnp.arange(pixel_flag.shape[1], dtype=jnp.int32) // strip_width
    covered = (strip_index[None, :] >= footprint[:, 0:1]) & (
        strip_index[None, :] <= footprint[:, 1:2]
    )
    return pixel_flag.astype(jnp.float32) * covered[:, :, None].astype(jnp.float32)


def partial_sums(weight, values, common_table, banded_table):
    common = jnp.einsum("dxy,dk->kxy", weight, common_table, precision=lax.Precision.HIGHEST)
    weighted = values.astype(jnp.float32) * weight[:, None]
    banded = jnp.einsum("dsxy,dk->ksxy", weighted, banded_table, precision=lax.Precision.HIGHEST)
    return (common, banded)


def solve_normal(gram, rhs):
    pair_list = [(row_term, col_term) for row_term in range(8) for col_term in range(row_term + 1)]
    gram_entry = {}
    for position, term_pair in enumerate(pair_list):
        gram_entry[term_pair] = gram[position]
    factor = {}
    for col_term in range(8):
        pivot_value = gram_entry[col_term, col_term] + RIDGE
        for inner_term in range(col_term):
            pivot_value = pivot_value - factor[col_term, inner_term] * factor[col_term, inner_term]
        diag_root = jnp.sqrt(pivot_value)
        factor[col_term, col_term] = diag_root
        for row_term in range(col_term + 1, 8):
            running = gram_entry[row_term, col_term]
            for inner_term in range(col_term):
                running = running - factor[row_term, inner_term] * factor[col_term, inner_term]
            factor[row_term, col_term] = running / diag_root
    forward = []
    for row_term in range(8):
        running = rhs[row_term]
        for inner_term in range(row_term):
            running = running - factor[row_term, inner_term] * forward[inner_term]
        forward.append(running / factor[row_term, row_term])
    backward = [forward[0]] * 8
    for row_term in reversed(range(8)):
        running = forward[row_term]
        for inner_term in range(row_term + 1, 8):
            running = running - factor[inner_term, row_term] * backward[inner_term]
        backward[row_term] = running / factor[row_term, row_term]
    return jnp.stack(backward, axis=0)


def smooth_axis(padded_field, along):
    inner_size = padded_field.shape[along] - 2
    left_part = lax.slice_in_dim(padded_field, 0, inner_size, axis=along)
    centre_part = lax.slice_in_dim(padded_field, 1, inner_size + 1, axis=along)
    right_part = lax.slice_in_dim(padded_field, 2, inner_size + 2, axis=along)
    return 0.25 * left_part + 0.5 * centre_part + 0.25 * right_part


def shards(scenes, clear_bits, footprint, offsets, acq_day):
    date_count, band_count, row_local, col_count = scenes.shape
    strip_count = lax.axis_size("band")
    tile_count = lax.axis_size("tile")
    strip_width = col_count // strip_count
    row_count = row_local * strip_count
    common_table, banded_table = design_tables(acq_day)
    below = shifted(scenes[:, :, 0:1, :], "band", -1)
    resampled = bilinear(jnp.concatenate([scenes, below], axis=2), offsets)
    flipped = jnp.swapaxes(resampled, 2, 3)
    cell_words = lax.all_to_all(clear_bits, "band", split_axis=2, concat_axis=1, tiled=True)
    weight = clear_weight(cell_words, footprint, strip_width)
    common, banded = partial_sums(weight, flipped, common_table, banded_table)
    common, banded = (
        lax.all_to_all(common, "band", split_axis=1, concat_axis=2, tiled=True),
        lax.all_to_all(
            banded.reshape(-1, col_count, row_local),
            "band",
            split_axis=1,
            concat_axis=2,
            tiled=True,
        ),
    )
    banded = banded.reshape(20, band_count, strip_width, row_count)
    gram = common[:36]
    month_count = common[36:]
    rhs = banded[:8]
    month_sum = banded[8:]
    annual_sum = jnp.sum(month_sum, axis=0)
    annual_count = jnp.sum(month_count, axis=0)
    month_sum, month_count = (
        lax.psum_scatter(month_sum, "tile", scatter_dimension=0, tiled=True),
        lax.psum_scatter(month_count, "tile", scatter_dimension=0, tiled=True),
    )
    composite = month_sum / jnp.maximum(month_count, 1.0)[:, None]
    month_edged = extended(composite, (("band", 2),), 1)
    month_edged = jnp.pad(month_edged, ((0, 0), (0, 0), (0, 0), (1, 1)))
    monthly = smooth_axis(smooth_axis(month_edged, 3), 2)
    share = row_count // tile_count
    gram, rhs, annual_sum, annual_count = lax.psum((gram, rhs, annual_sum, annual_count), "tile")
    start = lax.axis_index("tile") * share
    gram = lax.dynamic_slice_in_dim(gram, start, share, 2)
    rhs = lax.dynamic_slice_in_dim(rhs, start, share, 3)
    annual_sum = lax.dynamic_slice_in_dim(annual_sum, start, share, 2)
    annual_count = lax.dynamic_slice_in_dim(annual_count, start, share, 1)
    coefficients = solve_normal(gram, rhs)
    yearly = annual_sum / jnp.maximum(annual_count, 1.0)
    year_edged = extended(yearly, (("band", 1), ("tile", 2)), 1)
    annual = smooth_axis(smooth_axis(year_edged, 2), 1)
    return (coefficients, monthly, annual)


def fit_kernel(dates, bands, strips, off, foot, day_s, day_v, words, scenes, out,
               scn, hsf, hs, hr, bits, mix, mix_last, wide, w8, tables, edge_x, edge_w, fac, stack, planes, send,
               scene_sem, bit_send, bit_recv, halo_sem, blk_send, blk_recv, own_sem):
    f32, bf16, i32 = jnp.float32, jnp.bfloat16, jnp.int32
    me = lax.axis_index("band")
    sub8 = lax.broadcasted_iota(i32, (8, 128), 0)
    lane8 = lax.broadcasted_iota(i32, (8, 128), 1)
    upper = sub8 < 4
    depth = dates * 8
    load = pltpu.make_async_copy(scenes, scn, scene_sem)
    load.start()

    def at(k):
        return lax.rem(me + k, strips)

    barrier = pltpu.get_barrier_semaphore()

    def greet(k, c):
        pl.semaphore_signal(barrier, inc=1, device_id={"band": at(k)}, device_id_type=pl.DeviceIdType.MESH)
        return c

    lax.fori_loop(1, strips, greet, 0)
    pl.semaphore_wait(barrier, strips - 1)

    def bit_copy(k):
        return pltpu.make_async_remote_copy(
            src_ref=words, dst_ref=bits.at[me], send_sem=bit_send.at[at(k)], recv_sem=bit_recv.at[me],
            device_id={"band": at(k)}, device_id_type=pl.DeviceIdType.MESH)

    def send_bits(k, c):
        bit_copy(k).start()
        return c

    lax.fori_loop(1, strips, send_bits, 0)
    own_bits = pltpu.make_async_copy(words, bits.at[me], own_sem.at[0])
    own_bits.start()

    def basis(day, shape, which):
        u = day.astype(f32) / 365.0
        h = (which // 2).astype(f32)
        wave = jnp.cos((2.0 * jnp.pi) * h * u - jnp.where(which % 2 == 1, 0.5 * jnp.pi, 0.0))
        return jnp.where(which == 0, 1.0, jnp.where(which == 1, 2.0 * u - 1.0, wave))

    d8 = jnp.broadcast_to(day_v[...], (8, 64))
    which8 = lax.broadcasted_iota(i32, (8, 64), 0)
    real = lax.broadcasted_iota(i32, (8, 64), 1) < dates
    b8 = jnp.where(real, basis(d8, (8, 64), which8), 0.0)
    high = b8.astype(bf16).astype(f32)
    d16 = jnp.broadcast_to(day_v[...], (16, 64)) * 12
    m16 = lax.broadcasted_iota(i32, (16, 64), 0)
    ok16 = (lax.broadcasted_iota(i32, (16, 64), 1) < dates) & (m16 < 12)
    hot = jnp.where(ok16 & (d16 >= 365 * m16) & (d16 < 365 * m16 + 365), 1.0, 0.0)
    tab_in = jnp.concatenate([high, b8 - high, hot], axis=0).astype(bf16)
    choose = (lax.broadcasted_iota(i32, (224, 32), 0) // 8 == lax.broadcasted_iota(i32, (224, 32), 1)).astype(f32).astype(bf16)
    tab = jnp.dot(choose, tab_in, preferred_element_type=f32)
    last = lax.broadcasted_iota(i32, (224, 64), 0) % 8 == 7
    mix_last[...] = jnp.where(last, tab, 0.0).astype(bf16)
    place = (lax.broadcasted_iota(i32, (64, depth), 1) // 8 == lax.broadcasted_iota(i32, (64, depth), 0)).astype(f32).astype(bf16)
    full = jnp.dot(tab.astype(bf16), place, preferred_element_type=f32)
    same = lax.broadcasted_iota(i32, (224, depth), 0) % 8 == lax.broadcasted_iota(i32, (224, depth), 1) % 8
    mix[...] = jnp.where(same, full, 0.0).astype(bf16)
    planes[pl.ds(bands * 21 * 32, 64), :] = jnp.zeros((64, 128), f32)
    edge_x[...] = jnp.zeros((64, 128), f32)
    edge_w[...] = jnp.zeros((64, 128), f32)
    hsf[...] = jnp.zeros((bands, 64, 128), f32)

    load.wait()

    def first_rows(t, c):
        for s in range(bands):
            hsf[s, pl.ds(t, 1), :] = scn[t, s, 0:1, :].astype(f32)
        return c

    lax.fori_loop(0, dates, first_rows, 0, unroll=2)
    hs[...] = hsf[...].astype(bf16)
    halo = pltpu.make_async_remote_copy(
        src_ref=hs, dst_ref=hr, send_sem=halo_sem.at[0], recv_sem=halo_sem.at[1],
        device_id={"band": lax.rem(me + strips - 1, strips)}, device_id_type=pl.DeviceIdType.MESH)
    halo.start()

    def take_bits(k, c):
        pltpu.make_async_remote_copy(
            src_ref=words, dst_ref=bits.at[at(k)], send_sem=bit_send.at[at(k)], recv_sem=bit_recv.at[at(k)],
            device_id={"band": at(k)}, device_id_type=pl.DeviceIdType.MESH).wait()
        return c

    lax.fori_loop(1, strips, take_bits, 0)
    own_bits.wait()

    repeat = (lax.broadcasted_iota(i32, (128, strips), 0) // 4 == lax.broadcasted_iota(i32, (128, strips), 1)).astype(f32)
    cells = []
    for w in range(words.shape[0]):
        mine = pltpu.roll(bits[:, w, :], lax.rem(8 * (strips - me), 8 * strips), 1)[:, :128]
        parts = []
        for half in (mine & 32767, mine >> 15):
            spreadc = jnp.dot(repeat, half.astype(f32), precision=lax.Precision.HIGHEST, preferred_element_type=f32)
            parts.append(spreadc.T[0:8].astype(i32))
        cells.append(parts[0] + parts[1] * 32768)

    def spread(cell, rb):
        return jnp.where(upper, cell[2 * rb : 2 * rb + 1, :], cell[2 * rb + 1 : 2 * rb + 2, :])

    acc = tuple(jnp.zeros((8, 128), f32) for _ in range(48))
    for w in range(words.shape[0]):

        def date(j, acc):
            t = 30 * w + j
            seen = (lane8 >= 4 * foot[2 * t]) & (lane8 < 4 * foot[2 * t + 1] + 4)
            wt = jnp.where(seen, (cells[w] >> j) & 1, 0).astype(f32)
            fy = off[2 * t].astype(f32) * 0.0625
            fx = off[2 * t + 1].astype(f32) * 0.0625
            edge_x[pl.ds(t, 1), :] = jnp.full((1, 128), fx)
            edge_w[pl.ds(t, 1), :] = wt[7:8, :] * fy
            for rb in range(4):
                wide[t, pl.ds(8 * rb, 8), :] = spread(wt, rb)
            day = jnp.full((8, 128), day_s[t], i32)
            tables[0] = basis(day, (8, 128), sub8)
            b = [jnp.broadcast_to(tables[0, i : i + 1, :], (8, 128)) for i in range(8)]
            res = []
            for i in range(8):
                wb = wt * b[i]
                for k in range(i + 1):
                    res.append(acc[len(res)] + wb * b[k])
            d12 = day * 12
            for m in range(12):
                res.append(acc[len(res)] + jnp.where((d12 >= 365 * m) & (d12 < 365 * m + 365), wt, 0.0))
            return tuple(res)

        acc = lax.fori_loop(0, min(30, dates - 30 * w), date, acc)
    gram = {}
    for i in range(8):
        for j in range(i + 1):
            gram[i, j] = acc[i * (i + 1) // 2 + j]
    low, inv = {}, {}
    for j in range(8):
        pivot = gram[j, j] + RIDGE
        for k in range(j):
            pivot = pivot - low[j, k] * low[j, k]
        inv[j] = 1.0 / jnp.sqrt(pivot)
        for i in range(j + 1, 8):
            run = gram[i, j]
            for k in range(j):
                run = run - low[i, k] * low[j, k]
            low[i, j] = run * inv[j]
    items = [inv[i] for i in range(8)]
    items += [low[i, j] for i in range(8) for j in range(i)]
    items += [1.0 / jnp.maximum(acc[36 + m], 1.0) for m in range(12)]
    total = acc[36]
    for m in range(1, 12):
        total = total + acc[36 + m]
    items.append(1.0 / jnp.maximum(total, 1.0))
    for n, item in enumerate(items):
        for rb in range(4):
            fac[n, pl.ds(8 * rb, 8), :] = spread(item, rb)

    halo.wait()

    @pl.when(me == strips - 1)
    def _():
        hr[...] = jnp.zeros((bands, 64, 128), bf16)

    lane = lax.broadcasted_iota(i32, (32, 128), 1)
    row = lax.broadcasted_iota(i32, (32, 128), 0)
    lane64 = lax.broadcasted_iota(i32, (64, 128), 1)
    ends = jnp.where(lane8 > 0, 0.25, 0.0), jnp.where(lane8 < 127, 0.25, 0.0)
    first = lax.broadcasted_iota(i32, (16, 8, 128), 1) < 4
    groups = send.shape[2] // 16

    def smooth(x):
        return 0.5 * x + ends[0] * pltpu.roll(x, 1, 1) + ends[1] * pltpu.roll(x, 127, 1)

    def band(s, carry):
        def pair(p, c):
            u = []
            for t2 in range(2):
                t = 2 * p + t2
                fy = off[2 * t].astype(f32) * 0.0625
                fx = off[2 * t + 1].astype(f32) * 0.0625
                x = scn[t, s].astype(f32)
                xb = (1.0 - fx) * x + jnp.where(lane < 127, fx, 0.0) * pltpu.roll(x, 127, 1)
                v = (1.0 - fy) * xb + jnp.where(row < 31, fy, 0.0) * pltpu.roll(xb, 31, 0)
                u.append(v * wide[t])
            for rb in range(4):
                both = jnp.concatenate([u[0][8 * rb : 8 * rb + 8], u[1][8 * rb : 8 * rb + 8]], axis=0)
                stack[rb // 2, pl.ds(pl.multiple_of(16 * p, 16), 16), pl.ds(128 * (rb % 2), 128)] = both.astype(bf16)
            return c

        lax.fori_loop(0, dates // 2, pair, 0, unroll=2)
        e = hr[s].astype(f32)
        fx = edge_x[...]
        hu = ((1.0 - fx) * e + jnp.where(lane64 < 127, fx, 0.0) * pltpu.roll(e, 127, 1)) * edge_w[...]
        sums = [jnp.dot(mix[...], stack[h], preferred_element_type=f32) for h in range(2)]
        extra = jnp.dot(mix_last[...], hu.astype(bf16), preferred_element_type=f32)
        for rb in range(4):
            rows = pl.ds(8 * rb, 8)

            def term(n):
                part = sums[rb // 2][8 * n : 8 * n + 8, 128 * (rb % 2) : 128 * (rb % 2) + 128]
                return part + extra[8 * n : 8 * n + 8] if rb == 3 else part

            def fl(i, j):
                return fac[8 + i * (i - 1) // 2 + j, rows, :]

            def put(n, value):
                start = pl.multiple_of((s * 21 + n) * 32 + 8 * rb, 8)
                planes[pl.ds(start, 8), :] = value

            fwd = []
            for i in range(8):
                run = term(i) + term(8 + i)
                for k in range(i):
                    run = run - fl(i, k) * fwd[k]
                fwd.append(run * fac[i, rows, :])
            back = [None] * 8
            for i in reversed(range(8)):
                run = fwd[i]
                for k in range(i + 1, 8):
                    run = run - fl(k, i) * back[k]
                back[i] = run * fac[i, rows, :]
                put(i, back[i])
            whole = None
            for m in range(12):
                month = term(16 + m)
                whole = month if whole is None else whole + month
                put(8 + m, smooth(month * fac[36 + m, rows, :]))
            put(20, smooth(whole * fac[48, rows, :]))

        def group(gg, c):
            at16 = pl.ds(pl.multiple_of(16 * gg, 16), 16)
            halves = []
            for h in range(2):
                a, b = [
                    planes[pl.ds(pl.multiple_of((4 * gg + 2 * h + k) * 128, 128), 128), :].T.reshape(16, 8, 128)
                    for k in range(2)
                ]
                halves.append((jnp.where(first, a, pltpu.roll(b, 4, 1)), jnp.where(first, pltpu.roll(a, 4, 1), b)))
            for which in range(2):
                send[:, which, at16, :] = jnp.concatenate([halves[0][which], halves[1][which]], axis=1).astype(bf16)

            def push(k, c2):
                d = at(k)
                pltpu.make_async_remote_copy(
                    src_ref=send.at[d // 2, d % 2, at16, :], dst_ref=out.at[me, at16, :],
                    send_sem=blk_send.at[d], recv_sem=blk_recv.at[me],
                    device_id={"band": d}, device_id_type=pl.DeviceIdType.MESH).start()
                return c2

            lax.fori_loop(1, strips, push, 0)
            return c

        done = jnp.where(s == bands - 1, groups, (21 * (s + 1)) // 16)
        lax.fori_loop((21 * s) // 16, done, group, 0)
        return carry

    lax.fori_loop(0, bands, band, 0)
    own = pltpu.make_async_copy(send.at[me // 2, me % 2], out.at[me], own_sem.at[1])
    own.start()

    def finish(k, c):
        d = at(k)
        pltpu.make_async_remote_copy(
            src_ref=send.at[d // 2, d % 2], dst_ref=out.at[d], send_sem=blk_send.at[d], recv_sem=blk_recv.at[d],
            device_id={"band": d}, device_id_type=pl.DeviceIdType.MESH).wait()
        return c

    lax.fori_loop(1, strips, finish, 0)
    own.wait()


def lay_kernel(bands, recv, coef, monthly, annual):
    f32 = jnp.float32
    strips = recv.shape[0]
    quads = strips // 4
    width = strips * 32
    lane = lax.broadcasted_iota(jnp.int32, (8, 128), 1)
    even = (lane // 32) % 2 == 0
    front = lane < 64
    wide = lax.broadcasted_iota(jnp.int32, (8, width), 1)

    def swap(a, b, mask, shift):
        return jnp.where(mask, a, pltpu.roll(b, shift, 1)), jnp.where(mask, pltpu.roll(a, 128 - shift, 1), b)

    for gg in range(recv.shape[1] // 8):
        rows = [[], [], [], []]
        for q in range(quads):
            v = [recv[4 * q + j, pl.ds(8 * gg, 8), :].astype(f32) for j in range(4)]
            a0, a1 = swap(v[0], v[1], even, 32)
            a2, a3 = swap(v[2], v[3], even, 32)
            o0, o2 = swap(a0, a2, front, 64)
            o1, o3 = swap(a1, a3, front, 64)
            for p, o in enumerate((o0, o1, o2, o3)):
                rows[p].append(o)
        for p in range(4):
            full = jnp.concatenate(rows[p], axis=1)
            where_to = [divmod(4 * (2 * gg + half) + p, 21) for half in range(2)]
            if any(s < bands and j >= 8 for s, j in where_to):
                before = jnp.where(wide > 0, pltpu.roll(full, 1, 1), 0.0)
                after = jnp.where(wide < width - 1, pltpu.roll(full, width - 1, 1), 0.0)
                soft = 0.25 * before + 0.5 * full + 0.25 * after
            for half, (s, j) in enumerate(where_to):
                if s >= bands:
                    continue
                part = slice(4 * half, 4 * half + 4)
                if j < 8:
                    coef[j, s] = full[part]
                elif j < 20:
                    monthly[j - 8, s] = soft[part]
                else:
                    annual[s] = soft[part]


def fast(scenes, clear_bits, footprint, offsets, acq_day):
    f32, bf16 = jnp.float32, jnp.bfloat16
    dates, bands, rows, cols = scenes.shape
    strips = lax.axis_size("band")
    strip_width = cols // strips
    slots = -(-bands * 21 // 16) * 16
    smem = pl.BlockSpec(memory_space=pltpu.SMEM)
    vmem = pl.BlockSpec(memory_space=pltpu.VMEM)
    hbm = pl.BlockSpec(memory_space=pl.ANY)
    dma = pltpu.SemaphoreType.DMA
    words = clear_bits.reshape(clear_bits.shape[0], -1)
    recv = pl.pallas_call(
        functools.partial(fit_kernel, dates, bands, strips),
        out_shape=jax.ShapeDtypeStruct((strips, slots, cols), bf16),
        in_specs=[smem, smem, smem, vmem, vmem, hbm],
        out_specs=hbm,
        scratch_shapes=[
            pltpu.VMEM((dates, bands, rows, cols), bf16),
            pltpu.VMEM((bands, 64, cols), f32),
            pltpu.VMEM((bands, 64, cols), bf16),
            pltpu.VMEM((bands, 64, cols), bf16),
            pltpu.VMEM((strips,) + words.shape, jnp.int32),
            pltpu.VMEM((224, dates * 8), bf16),
            pltpu.VMEM((224, 64), bf16),
            pltpu.VMEM((dates, rows, cols), f32),
            pltpu.VMEM((8, cols), f32),
            pltpu.VMEM((1, 8, cols), f32),
            pltpu.VMEM((64, cols), f32),
            pltpu.VMEM((64, cols), f32),
            pltpu.VMEM((49, rows, cols), f32),
            pltpu.VMEM((2, dates * 8, 2 * cols), bf16),
            pltpu.VMEM((slots * rows, cols), f32),
            pltpu.VMEM((strips // 2, 2, slots, cols), bf16),
            dma, dma((strips,)), dma((strips,)), dma((2,)), dma((strips,)), dma((strips,)), dma((2,)),
        ],
        compiler_params=pltpu.CompilerParams(collective_id=0, has_side_effects=True, vmem_limit_bytes=48 * 1024 * 1024),
    )(offsets.reshape(-1), footprint.reshape(-1), acq_day, jnp.pad(acq_day, (0, 64 - dates))[None], words, scenes)
    return pl.pallas_call(
        functools.partial(lay_kernel, bands),
        out_shape=(
            jax.ShapeDtypeStruct((8, bands, strip_width, rows * strips), f32),
            jax.ShapeDtypeStruct((12, bands, strip_width, rows * strips), f32),
            jax.ShapeDtypeStruct((bands, strip_width, rows * strips), f32),
        ),
        in_specs=[vmem],
        out_specs=(vmem, vmem, vmem),
        compiler_params=pltpu.CompilerParams(vmem_limit_bytes=32 * 1024 * 1024),
    )(recv)


def pick(scenes, clear_bits, footprint, offsets, acq_day):
    dates, bands, rows, cols = scenes.shape
    strips = lax.axis_size("band")
    fits = lax.axis_size("tile") == 1 and lax.axis_size("sub") == 1 and strips % 4 == 0
    fits = fits and cols == 128 and rows == 32 and cols == 4 * strips and dates % 2 == 0 and dates <= 60
    return (fast if fits else shards)(scenes, clear_bits, footprint, offsets, acq_day)


def solution(mesh):
    placed = (
        P(("region", "tile"), "sub", "band", None),
        P(("region", "tile"), "band", None),
        P(("region", "tile"), None),
        P(("region", "tile"), None),
        P(("region", "tile")),
    )
    return jax.shard_map(
        pick,
        mesh=mesh,
        in_specs=placed,
        out_specs=(
            P("region", "sub", "band", "tile"),
            P(("region", "tile"), "sub", "band", None),
            P(("region", "sub"), "band", "tile"),
        ),
        check_vma=False,
    )
```

profile of v0, /device:TPU:0, one launch (start us, length us, event | category | flops | bytes accessed | tf_op | source)
XLA Modules:
  0.0 62.8 jit_solution(17640545129257640120)
XLA Ops:
  0.6 0.7 %pad_bitcast_fusion.day_v = s32[1,64]{1,0:T(1,128)S(1)} fusion(s32[60]{0:T(128)} %day_s.1), kind=kLoop, calls=%fused_computation.1 | loop fusion | bytes 496 | tf_op jit(solution)/shard_map/broadcast_in_dim | solution.py:529
  1.3 0.7 %copy.14 = s32[2,1,256]{2,0,1:T(2,128)S(1)} copy(s32[2,1,256]{2,1,0:T(1,128)} %param.6) | data formatting | bytes 4096
  2.0 0.8 %copy.11 = s32[60,2]{1,0:T(8,128)S(1)} copy(s32[60,2]{0,1:T(2,128)} %param.7) | data formatting | bytes 960 | tf_op args[2]
  2.8 0.1 reshape.16.foot
  2.9 0.8 %copy.10 = s32[60,2]{1,0:T(8,128)S(1)} copy(s32[60,2]{0,1:T(2,128)} %param.8) | data formatting | bytes 960 | tf_op args[3]
  3.7 0.1 reshape.15.off
  3.8 0.0 copy-start
  3.8 1.8 %copy-done = bf16[60,6,32,128]{3,2,1,0:T(8,128)(2,1)S(1)} copy-done((bf16[60,6,32,128]{3,2,1,0:T(8,128)(2,1)S(1)}, bf16[60,6,32,128]{3,2,1,0:T(8,128)(2,1)}, u32[]{:S(2)}) %copy-start) | copy-done | bytes 2949144
  5.6 0.0 copy-start.1
  5.6 0.7 %copy-done.1 = s32[60]{0:T(128)S(1)} copy-done((s32[60]{0:T(128)S(1)}, s32[60]{0:T(128)}, u32[]{:S(2)}) %copy-start.1) | copy-done | bytes 264
  6.3 46.2 %shard_map.76.recv = bf16[32,128,128]{2,1,0:T(8,128)(2,1)S(1)} custom-call(s32[120]{0:T(128)S(1)} %reshape.15.off, s32[120]{0:T(128)S(1)} %reshape.16.foot, s32[60]{0:T(128)S(1)} %copy-done.1, s32[1,64]{1,0:T(1,128)S(1)} %pad_bitcast_fusion.day_v, s32[2,256]{1,0:T(2,128)S(1)} %bitcast.5, bf16[60,6,32,128]{3,2,1,0:T(8,128)(2,1)S(1)} %copy-done), custom_call_target="tpu_custom_call" | custom-call | tf_op jit(solution)/shard_map/pallas_call | solution.py:504
  52.5 10.3 %shard_map.77 = (f32[8,6,4,1024]{3,2,1,0:T(4,128)}, f32[12,6,4,1024]{3,2,1,0:T(4,128)}, f32[6,4,1024]{2,1,0:T(4,128)}) custom-call(bf16[32,128,128]{2,1,0:T(8,128)(2,1)S(1)} %shard_map.76.recv), custom_call_target="tpu_custom_call" | custom-call | tf_op jit(solution)/shard_map/pallas_call | solution.py:530
Async XLA Ops:
  3.8 1.8 %copy-start = (bf16[60,6,32,128]{3,2,1,0:T(8,128)(2,1)S(1)}, bf16[60,6,32,128]{3,2,1,0:T(8,128)(2,1)}, u32[]{:S(2)}) copy-start(bf16[60,6,32,128]{3,2,1,0:T(8,128)(2,1)} %scenes.1) | copy-start | bytes 8847364
  5.6 0.7 %copy-start.1 = (s32[60]{0:T(128)S(1)}, s32[60]{0:T(128)}, u32[]{:S(2)}) copy-start(s32[60]{0:T(128)} %day_s.1) | copy-start | bytes 724
where the time goes:
time: 63 us; the launch traced here: 62.8 us
  Pallas kernels  56.5 us (90%)
  local copies, waits for them, and re-layouts  5.65 us (9%)
  between operations  0.65 us (1%)
    pallas_call x1, Pallas kernels, fast(): pl.pallas_call(functools.partial(fit_kernel, dates, bands, strips), out_s...  46.2 us
    pallas_call x1, Pallas kernels, fast(): pl.pallas_call(functools.partial(lay_kernel, bands), out_shape=(jax.Shape...  10.3 us
    unnamed x7, local copies, waits for them, and re-layouts  4.73 us

commit v1 on v0

--- a/solution.py
+++ b/solution.py
@@ -1,4 +1,5 @@
 import functools
+import math
 
 import jax
 import jax.numpy as jnp
@@ -179,8 +180,8 @@
     return (coefficients, monthly, annual)
 
 
-def fit_kernel(dates, bands, strips, off, foot, day_s, day_v, words, scenes, out,
-               scn, hsf, hs, hr, bits, mix, mix_last, wide, w8, tables, edge_x, edge_w, fac, stack, planes, send,
+def fit_kernel(dates, bands, strips, off, foot, day_s, words, scenes, out,
+               scn, hsf, hs, hr, bits, mix, mix_last, wide, tables, edge_x, edge_w, fac, stack, planes, send,
                scene_sem, bit_send, bit_recv, halo_sem, blk_send, blk_recv, own_sem):
     f32, bf16, i32 = jnp.float32, jnp.bfloat16, jnp.int32
     me = lax.axis_index("band")
@@ -194,6 +195,12 @@
     def at(k):
         return lax.rem(me + k, strips)
 
+    half = strips // 2
+
+    def peer(k):
+        cross = (me // half + 1 + k // half) % 2
+        return cross * half + (me + k) % half
+
     barrier = pltpu.get_barrier_semaphore()
 
     def greet(k, c):
@@ -201,33 +208,29 @@
         return c
 
     lax.fori_loop(1, strips, greet, 0)
-    pl.semaphore_wait(barrier, strips - 1)
-
-    def bit_copy(k):
-        return pltpu.make_async_remote_copy(
-            src_ref=words, dst_ref=bits.at[me], send_sem=bit_send.at[at(k)], recv_sem=bit_recv.at[me],
-            device_id={"band": at(k)}, device_id_type=pl.DeviceIdType.MESH)
-
-    def send_bits(k, c):
-        bit_copy(k).start()
-        return c
-
-    lax.fori_loop(1, strips, send_bits, 0)
-    own_bits = pltpu.make_async_copy(words, bits.at[me], own_sem.at[0])
-    own_bits.start()
-
-    def basis(day, shape, which):
+
+    def basis(day, which):
         u = day.astype(f32) / 365.0
-        h = (which // 2).astype(f32)
-        wave = jnp.cos((2.0 * jnp.pi) * h * u - jnp.where(which % 2 == 1, 0.5 * jnp.pi, 0.0))
+        turn = (which // 2).astype(f32) * u - jnp.where(which % 2 == 1, 0.25, 0.0)
+        turn = turn - jnp.floor(turn + 0.5)
+        square = (turn * turn) * (4.0 * math.pi * math.pi)
+        wave = jnp.full_like(square, 1.0 / math.factorial(20))
+        for k in range(9, -1, -1):
+            wave = (-1.0) ** k / math.factorial(2 * k) + wave * square
         return jnp.where(which == 0, 1.0, jnp.where(which == 1, 2.0 * u - 1.0, wave))
 
-    d8 = jnp.broadcast_to(day_v[...], (8, 64))
+    lane64i = lax.broadcasted_iota(i32, (16, 64), 1)
+
+    def days(t, acc):
+        return jnp.where(lane64i == t, day_s[t], acc)
+
+    day64 = lax.fori_loop(0, dates, days, jnp.zeros((16, 64), i32), unroll=10)
+    d8 = day64[0:8]
     which8 = lax.broadcasted_iota(i32, (8, 64), 0)
     real = lax.broadcasted_iota(i32, (8, 64), 1) < dates
-    b8 = jnp.where(real, basis(d8, (8, 64), which8), 0.0)
+    b8 = jnp.where(real, basis(d8, which8), 0.0)
     high = b8.astype(bf16).astype(f32)
-    d16 = jnp.broadcast_to(day_v[...], (16, 64)) * 12
+    d16 = day64 * 12
     m16 = lax.broadcasted_iota(i32, (16, 64), 0)
     ok16 = (lax.broadcasted_iota(i32, (16, 64), 1) < dates) & (m16 < 12)
     hot = jnp.where(ok16 & (d16 >= 365 * m16) & (d16 < 365 * m16 + 365), 1.0, 0.0)
@@ -245,6 +248,30 @@
     edge_w[...] = jnp.zeros((64, 128), f32)
     hsf[...] = jnp.zeros((bands, 64, 128), f32)
 
+    sub16 = lax.broadcasted_iota(i32, (16, 128), 0)
+
+    def date_tables(t, c):
+        tables[t, 0:8, :] = basis(jnp.full((8, 128), day_s[t], i32), sub8)
+        d12 = jnp.full((16, 128), day_s[t], i32) * 12
+        tables[t, 8:24, :] = jnp.where((d12 >= 365 * sub16) & (d12 < 365 * sub16 + 365), 1.0, 0.0)
+        return c
+
+    lax.fori_loop(0, dates, date_tables, 0, unroll=6)
+    pl.semaphore_wait(barrier, strips - 1)
+
+    def bit_copy(k):
+        return pltpu.make_async_remote_copy(
+            src_ref=words, dst_ref=bits.at[me], send_sem=bit_send.at[at(k)], recv_sem=bit_recv.at[me],
+            device_id={"band": at(k)}, device_id_type=pl.DeviceIdType.MESH)
+
+    def send_bits(k, c):
+        bit_copy(k).start()
+        return c
+
+    lax.fori_loop(1, strips, send_bits, 0)
+    own_bits = pltpu.make_async_copy(words, bits.at[me], own_sem.at[0])
+    own_bits.start()
+
     load.wait()
 
     def first_rows(t, c):
@@ -271,10 +298,10 @@
     repeat = (lax.broadcasted_iota(i32, (128, strips), 0) // 4 == lax.broadcasted_iota(i32, (128, strips), 1)).astype(f32)
     cells = []
     for w in range(words.shape[0]):
-        mine = pltpu.roll(bits[:, w, :], lax.rem(8 * (strips - me), 8 * strips), 1)[:, :128]
+        mine = pltpu.roll(bits[:, w, 0, :], lax.rem(8 * (strips - me), 8 * strips), 1)[:, :128]
         parts = []
-        for half in (mine & 32767, mine >> 15):
-            spreadc = jnp.dot(repeat, half.astype(f32), precision=lax.Precision.HIGHEST, preferred_element_type=f32)
+        for piece in (mine & 32767, mine >> 15):
+            spreadc = jnp.dot(repeat, piece.astype(f32), precision=lax.Precision.HIGHEST, preferred_element_type=f32)
             parts.append(spreadc.T[0:8].astype(i32))
         cells.append(parts[0] + parts[1] * 32768)
 
@@ -286,28 +313,25 @@
 
         def date(j, acc):
             t = 30 * w + j
-            seen = (lane8 >= 4 * foot[2 * t]) & (lane8 < 4 * foot[2 * t + 1] + 4)
+            seen = (lane8 >= 4 * foot[0, t]) & (lane8 < 4 * foot[1, t] + 4)
             wt = jnp.where(seen, (cells[w] >> j) & 1, 0).astype(f32)
-            fy = off[2 * t].astype(f32) * 0.0625
-            fx = off[2 * t + 1].astype(f32) * 0.0625
+            fy = off[0, t].astype(f32) * 0.0625
+            fx = off[1, t].astype(f32) * 0.0625
             edge_x[pl.ds(t, 1), :] = jnp.full((1, 128), fx)
             edge_w[pl.ds(t, 1), :] = wt[7:8, :] * fy
             for rb in range(4):
                 wide[t, pl.ds(8 * rb, 8), :] = spread(wt, rb)
-            day = jnp.full((8, 128), day_s[t], i32)
-            tables[0] = basis(day, (8, 128), sub8)
-            b = [jnp.broadcast_to(tables[0, i : i + 1, :], (8, 128)) for i in range(8)]
+            b = [jnp.broadcast_to(tables[t, i : i + 1, :], (8, 128)) for i in range(20)]
             res = []
             for i in range(8):
                 wb = wt * b[i]
                 for k in range(i + 1):
                     res.append(acc[len(res)] + wb * b[k])
-            d12 = day * 12
             for m in range(12):
-                res.append(acc[len(res)] + jnp.where((d12 >= 365 * m) & (d12 < 365 * m + 365), wt, 0.0))
+                res.append(acc[len(res)] + wt * b[8 + m])
             return tuple(res)
 
-        acc = lax.fori_loop(0, min(30, dates - 30 * w), date, acc)
+        acc = lax.fori_loop(0, min(30, dates - 30 * w), date, acc, unroll=2)
     gram = {}
     for i in range(8):
         for j in range(i + 1):
@@ -355,8 +379,8 @@
             u = []
             for t2 in range(2):
                 t = 2 * p + t2
-                fy = off[2 * t].astype(f32) * 0.0625
-                fx = off[2 * t + 1].astype(f32) * 0.0625
+                fy = off[0, t].astype(f32) * 0.0625
+                fx = off[1, t].astype(f32) * 0.0625
                 x = scn[t, s].astype(f32)
                 xb = (1.0 - fx) * x + jnp.where(lane < 127, fx, 0.0) * pltpu.roll(x, 127, 1)
                 v = (1.0 - fy) * xb + jnp.where(row < 31, fy, 0.0) * pltpu.roll(xb, 31, 0)
@@ -419,14 +443,15 @@
                 send[:, which, at16, :] = jnp.concatenate([halves[0][which], halves[1][which]], axis=1).astype(bf16)
 
             def push(k, c2):
-                d = at(k)
+                d = peer(k)
                 pltpu.make_async_remote_copy(
                     src_ref=send.at[d // 2, d % 2, at16, :], dst_ref=out.at[me, at16, :],
                     send_sem=blk_send.at[d], recv_sem=blk_recv.at[me],
                     device_id={"band": d}, device_id_type=pl.DeviceIdType.MESH).start()
                 return c2
 
-            lax.fori_loop(1, strips, push, 0)
+            lax.fori_loop(0, half, push, 0)
+            lax.fori_loop(half + 1, strips, push, 0)
             return c
 
         done = jnp.where(s == bands - 1, groups, (21 * (s + 1)) // 16)
@@ -448,7 +473,7 @@
     own.wait()
 
 
-def lay_kernel(bands, recv, coef, monthly, annual):
+def lay_kernel(bands, recv, coef_out, monthly_out, annual_out, coef, monthly, annual, sems):
     f32 = jnp.float32
     strips = recv.shape[0]
     quads = strips // 4
@@ -484,10 +509,16 @@
                 part = slice(4 * half, 4 * half + 4)
                 if j < 8:
                     coef[j, s] = full[part]
+                    pltpu.make_async_copy(coef.at[j, s], coef_out.at[j, s], sems.at[0]).start()
                 elif j < 20:
                     monthly[j - 8, s] = soft[part]
+                    pltpu.make_async_copy(monthly.at[j - 8, s], monthly_out.at[j - 8, s], sems.at[1]).start()
                 else:
                     annual[s] = soft[part]
+                    pltpu.make_async_copy(annual.at[s], annual_out.at[s], sems.at[2]).start()
+    pltpu.make_async_copy(coef, coef_out, sems.at[0]).wait()
+    pltpu.make_async_copy(monthly, monthly_out, sems.at[1]).wait()
+    pltpu.make_async_copy(annual, annual_out, sems.at[2]).wait()
 
 
 def fast(scenes, clear_bits, footprint, offsets, acq_day):
@@ -500,23 +531,21 @@
     vmem = pl.BlockSpec(memory_space=pltpu.VMEM)
     hbm = pl.BlockSpec(memory_space=pl.ANY)
     dma = pltpu.SemaphoreType.DMA
-    words = clear_bits.reshape(clear_bits.shape[0], -1)
     recv = pl.pallas_call(
         functools.partial(fit_kernel, dates, bands, strips),
         out_shape=jax.ShapeDtypeStruct((strips, slots, cols), bf16),
-        in_specs=[smem, smem, smem, vmem, vmem, hbm],
+        in_specs=[smem, smem, smem, vmem, hbm],
         out_specs=hbm,
         scratch_shapes=[
             pltpu.VMEM((dates, bands, rows, cols), bf16),
             pltpu.VMEM((bands, 64, cols), f32),
             pltpu.VMEM((bands, 64, cols), bf16),
             pltpu.VMEM((bands, 64, cols), bf16),
-            pltpu.VMEM((strips,) + words.shape, jnp.int32),
+            pltpu.VMEM((strips,) + clear_bits.shape, jnp.int32),
             pltpu.VMEM((224, dates * 8), bf16),
             pltpu.VMEM((224, 64), bf16),
             pltpu.VMEM((dates, rows, cols), f32),
-            pltpu.VMEM((8, cols), f32),
-            pltpu.VMEM((1, 8, cols), f32),
+            pltpu.VMEM((dates, 24, cols), f32),
             pltpu.VMEM((64, cols), f32),
             pltpu.VMEM((64, cols), f32),
             pltpu.VMEM((49, rows, cols), f32),
@@ -525,8 +554,8 @@
             pltpu.VMEM((strips // 2, 2, slots, cols), bf16),
             dma, dma((strips,)), dma((strips,)), dma((2,)), dma((strips,)), dma((strips,)), dma((2,)),
         ],
-        compiler_params=pltpu.CompilerParams(collective_id=0, has_side_effects=True, vmem_limit_bytes=48 * 1024 * 1024),
-    )(offsets.reshape(-1), footprint.reshape(-1), acq_day, jnp.pad(acq_day, (0, 64 - dates))[None], words, scenes)
+        compiler_params=pltpu.CompilerParams(collective_id=0, has_side_effects=True, vmem_limit_bytes=58 * 1024 * 1024),
+    )(offsets.T, footprint.T, acq_day, clear_bits, scenes)
     return pl.pallas_call(
         functools.partial(lay_kernel, bands),
         out_shape=(
@@ -535,8 +564,14 @@
             jax.ShapeDtypeStruct((bands, strip_width, rows * strips), f32),
         ),
         in_specs=[vmem],
-        out_specs=(vmem, vmem, vmem),
-        compiler_params=pltpu.CompilerParams(vmem_limit_bytes=32 * 1024 * 1024),
+        out_specs=(hbm, hbm, hbm),
+        scratch_shapes=[
+            pltpu.VMEM((8, bands, strip_width, rows * strips), f32),
+            pltpu.VMEM((12, bands, strip_width, rows * strips), f32),
+            pltpu.VMEM((bands, strip_width, rows * strips), f32),
+            dma((3,)),
+        ],
+        compiler_params=pltpu.CompilerParams(vmem_limit_bytes=56 * 1024 * 1024),
     )(recv)
 
 

time: 63 us -> 55.3 us (0.88)
  local copies, waits for them, and re-layouts: 5.65 us -> 0 us
  Pallas kernels: 56.5 us -> 54.5 us
    unnamed x7 -> x0, local copies, waits for them, and re-layouts: 4.73 us -> none
    pallas_call x1, Pallas kernels: 46.2 us -> 43.6 us  [fast(): pl.pallas_call(functools.partial(fit_kernel, dates, bands, strips), out_s...]
    broadcast_in_dim x1 -> x0, local copies, waits for them, and re-layouts: 0.66 us -> none  [fast(): jnp.pad(acq_day, (0, 64 - dates))[None]]
where the time goes in v1:
time: 55.3 us; the launch traced here: 55.1 us
  Pallas kernels  54.5 us (99%)
  between operations  0.64 us (1%)
    pallas_call x1, Pallas kernels, fast(): pl.pallas_call(functools.partial(fit_kernel, dates, bands, strips), out_s...  43.6 us
    pallas_call x1, Pallas kernels, fast(): pl.pallas_call(functools.partial(lay_kernel, bands), out_shape=(jax.Shape...  10.9 us

profile of v1, /device:TPU:0, one launch (start us, length us, event | category | flops | bytes accessed | tf_op | source)
XLA Modules:
  0.0 55.1 jit_solution(17664174483026779334)
XLA Ops:
  0.6 43.6 %shard_map.76.recv = bf16[32,128,128]{2,1,0:T(8,128)(2,1)} custom-call(s32[2,60]{1,0:T(2,128)} %bitcast.2, s32[2,60]{1,0:T(2,128)} %bitcast.3, s32[60]{0:T(128)} %day_s.1, s32[2,1,256]{2,1,0:T(1,128)} %words.1, bf16[60,6,32,128]{3,2,1,0:T(8,128)(2,1)} %scenes.1), custom_call_target="tpu_custom_call" | custom-call | tf_op jit(solution)/shard_map/pallas_call | solution.py:534
  44.3 10.9 %shard_map.77 = (f32[8,6,4,1024]{3,2,1,0:T(4,128)}, f32[12,6,4,1024]{3,2,1,0:T(4,128)}, f32[6,4,1024]{2,1,0:T(4,128)}) custom-call(bf16[32,128,128]{2,1,0:T(8,128)(2,1)} %shard_map.76.recv), custom_call_target="tpu_custom_call" | custom-call | tf_op jit(solution)/shard_map/pallas_call | solution.py:559

commit v2 on v1

--- a/solution.py
+++ b/solution.py
@@ -181,7 +181,7 @@
 
 
 def fit_kernel(dates, bands, strips, off, foot, day_s, words, scenes, out,
-               scn, hsf, hs, hr, bits, mix, mix_last, wide, tables, edge_x, edge_w, fac, stack, planes, send,
+               scn, hsf, hs, hr, bits, mix, mix_last, wide, mix_gram, cover, edge_x, edge_w, fac, stack, planes, send,
                scene_sem, bit_send, bit_recv, halo_sem, blk_send, blk_recv, own_sem):
     f32, bf16, i32 = jnp.float32, jnp.bfloat16, jnp.int32
     me = lax.axis_index("band")
@@ -243,20 +243,19 @@
     full = jnp.dot(tab.astype(bf16), place, preferred_element_type=f32)
     same = lax.broadcasted_iota(i32, (224, depth), 0) % 8 == lax.broadcasted_iota(i32, (224, depth), 1) % 8
     mix[...] = jnp.where(same, full, 0.0).astype(bf16)
+    pairs = jnp.concatenate([b8[i : i + 1] * b8[: i + 1] for i in range(8)] + [jnp.zeros((4, 64), f32)], axis=0)
+    high_pairs = pairs.astype(bf16).astype(f32)
+    tab_pairs = jnp.concatenate([high_pairs, pairs - high_pairs, hot], axis=0).astype(bf16)
+    choose = (lax.broadcasted_iota(i32, (768, 96), 0) // 8 == lax.broadcasted_iota(i32, (768, 96), 1)).astype(f32).astype(bf16)
+    tab = jnp.dot(choose, tab_pairs, preferred_element_type=f32)
+    full = jnp.dot(tab.astype(bf16), place, preferred_element_type=f32)
+    same = lax.broadcasted_iota(i32, (768, depth), 0) % 8 == lax.broadcasted_iota(i32, (768, depth), 1) % 8
+    mix_gram[...] = jnp.where(same, full, 0.0).astype(bf16)
     planes[pl.ds(bands * 21 * 32, 64), :] = jnp.zeros((64, 128), f32)
     edge_x[...] = jnp.zeros((64, 128), f32)
     edge_w[...] = jnp.zeros((64, 128), f32)
     hsf[...] = jnp.zeros((bands, 64, 128), f32)
 
-    sub16 = lax.broadcasted_iota(i32, (16, 128), 0)
-
-    def date_tables(t, c):
-        tables[t, 0:8, :] = basis(jnp.full((8, 128), day_s[t], i32), sub8)
-        d12 = jnp.full((16, 128), day_s[t], i32) * 12
-        tables[t, 8:24, :] = jnp.where((d12 >= 365 * sub16) & (d12 < 365 * sub16 + 365), 1.0, 0.0)
-        return c
-
-    lax.fori_loop(0, dates, date_tables, 0, unroll=6)
     pl.semaphore_wait(barrier, strips - 1)
 
     def bit_copy(k):
@@ -308,10 +307,9 @@
     def spread(cell, rb):
         return jnp.where(upper, cell[2 * rb : 2 * rb + 1, :], cell[2 * rb + 1 : 2 * rb + 2, :])
 
-    acc = tuple(jnp.zeros((8, 128), f32) for _ in range(48))
     for w in range(words.shape[0]):
 
-        def date(j, acc):
+        def date(j, c):
             t = 30 * w + j
             seen = (lane8 >= 4 * foot[0, t]) & (lane8 < 4 * foot[1, t] + 4)
             wt = jnp.where(seen, (cells[w] >> j) & 1, 0).astype(f32)
@@ -321,17 +319,13 @@
             edge_w[pl.ds(t, 1), :] = wt[7:8, :] * fy
             for rb in range(4):
                 wide[t, pl.ds(8 * rb, 8), :] = spread(wt, rb)
-            b = [jnp.broadcast_to(tables[t, i : i + 1, :], (8, 128)) for i in range(20)]
-            res = []
-            for i in range(8):
-                wb = wt * b[i]
-                for k in range(i + 1):
-                    res.append(acc[len(res)] + wb * b[k])
-            for m in range(12):
-                res.append(acc[len(res)] + wt * b[8 + m])
-            return tuple(res)
-
-        acc = lax.fori_loop(0, min(30, dates - 30 * w), date, acc, unroll=2)
+            cover[pl.ds(pl.multiple_of(8 * t, 8), 8), :] = wt
+            return c
+
+        lax.fori_loop(0, min(30, dates - 30 * w), date, 0, unroll=2)
+    sums = jnp.dot(mix_gram[...], cover[...].astype(bf16), preferred_element_type=f32)
+    acc = [sums[8 * n : 8 * n + 8] + sums[320 + 8 * n : 328 + 8 * n] for n in range(36)]
+    acc += [sums[640 + 8 * m : 648 + 8 * m] for m in range(12)]
     gram = {}
     for i in range(8):
         for j in range(i + 1):
@@ -473,7 +467,7 @@
     own.wait()
 
 
-def lay_kernel(bands, recv, coef_out, monthly_out, annual_out, coef, monthly, annual, sems):
+def lay_kernel(bands, recv, coef, monthly, annual, flat, sems):
     f32 = jnp.float32
     strips = recv.shape[0]
     quads = strips // 4
@@ -486,10 +480,10 @@
     def swap(a, b, mask, shift):
         return jnp.where(mask, a, pltpu.roll(b, shift, 1)), jnp.where(mask, pltpu.roll(a, 128 - shift, 1), b)
 
-    for gg in range(recv.shape[1] // 8):
+    def rows8(gg, carry):
         rows = [[], [], [], []]
         for q in range(quads):
-            v = [recv[4 * q + j, pl.ds(8 * gg, 8), :].astype(f32) for j in range(4)]
+            v = [recv[4 * q + j, pl.ds(pl.multiple_of(8 * gg, 8), 8), :].astype(f32) for j in range(4)]
             a0, a1 = swap(v[0], v[1], even, 32)
             a2, a3 = swap(v[2], v[3], even, 32)
             o0, o2 = swap(a0, a2, front, 64)
@@ -498,27 +492,39 @@
                 rows[p].append(o)
         for p in range(4):
             full = jnp.concatenate(rows[p], axis=1)
-            where_to = [divmod(4 * (2 * gg + half) + p, 21) for half in range(2)]
-            if any(s < bands and j >= 8 for s, j in where_to):
-                before = jnp.where(wide > 0, pltpu.roll(full, 1, 1), 0.0)
-                after = jnp.where(wide < width - 1, pltpu.roll(full, width - 1, 1), 0.0)
-                soft = 0.25 * before + 0.5 * full + 0.25 * after
-            for half, (s, j) in enumerate(where_to):
-                if s >= bands:
-                    continue
+            before = jnp.where(wide > 0, pltpu.roll(full, 1, 1), 0.0)
+            after = jnp.where(wide < width - 1, pltpu.roll(full, width - 1, 1), 0.0)
+            soft = 0.25 * before + 0.5 * full + 0.25 * after
+            for half in range(2):
+                index = 8 * gg + 4 * half + p
                 part = slice(4 * half, 4 * half + 4)
-                if j < 8:
-                    coef[j, s] = full[part]
-                    pltpu.make_async_copy(coef.at[j, s], coef_out.at[j, s], sems.at[0]).start()
-                elif j < 20:
-                    monthly[j - 8, s] = soft[part]
-                    pltpu.make_async_copy(monthly.at[j - 8, s], monthly_out.at[j - 8, s], sems.at[1]).start()
-                else:
-                    annual[s] = soft[part]
-                    pltpu.make_async_copy(annual.at[s], annual_out.at[s], sems.at[2]).start()
-    pltpu.make_async_copy(coef, coef_out, sems.at[0]).wait()
-    pltpu.make_async_copy(monthly, monthly_out, sems.at[1]).wait()
-    pltpu.make_async_copy(annual, annual_out, sems.at[2]).wait()
+                flat[index] = jnp.where(index % 21 < 8, full[part], soft[part])
+
+        def ship(n, c):
+            index = 8 * gg + n
+            s, j = index // 21, index % 21
+
+            @pl.when((s < bands) & (j < 8))
+            def _():
+                pltpu.make_async_copy(flat.at[index], coef.at[j, s], sems.at[0]).start()
+
+            @pl.when((s < bands) & (j >= 8) & (j < 20))
+            def _():
+                pltpu.make_async_copy(flat.at[index], monthly.at[j - 8, s], sems.at[1]).start()
+
+            @pl.when((s < bands) & (j == 20))
+            def _():
+                pltpu.make_async_copy(flat.at[index], annual.at[s], sems.at[2]).start()
+
+            return c
+
+        lax.fori_loop(0, 8, ship, 0)
+        return carry
+
+    lax.fori_loop(0, recv.shape[1] // 8, rows8, 0)
+    pltpu.make_async_copy(coef, coef, sems.at[0]).wait()
+    pltpu.make_async_copy(monthly, monthly, sems.at[1]).wait()
+    pltpu.make_async_copy(annual, annual, sems.at[2]).wait()
 
 
 def fast(scenes, clear_bits, footprint, offsets, acq_day):
@@ -545,7 +551,8 @@
             pltpu.VMEM((224, dates * 8), bf16),
             pltpu.VMEM((224, 64), bf16),
             pltpu.VMEM((dates, rows, cols), f32),
-            pltpu.VMEM((dates, 24, cols), f32),
+            pltpu.VMEM((768, dates * 8), bf16),
+            pltpu.VMEM((dates * 8, cols), f32),
             pltpu.VMEM((64, cols), f32),
             pltpu.VMEM((64, cols), f32),
             pltpu.VMEM((49, rows, cols), f32),
@@ -566,9 +573,7 @@
         in_specs=[vmem],
         out_specs=(hbm, hbm, hbm),
         scratch_shapes=[
-            pltpu.VMEM((8, bands, strip_width, rows * strips), f32),
-            pltpu.VMEM((12, bands, strip_width, rows * strips), f32),
-            pltpu.VMEM((bands, strip_width, rows * strips), f32),
+            pltpu.VMEM((slots, strip_width, rows * strips), f32),
             dma((3,)),
         ],
         compiler_params=pltpu.CompilerParams(vmem_limit_bytes=56 * 1024 * 1024),

time: 55.3 us -> 53 us (0.958)
  Pallas kernels: 54.5 us -> 52.1 us
    pallas_call x1, Pallas kernels: 10.9 us -> 9.09 us  [fast(): pl.pallas_call(functools.partial(lay_kernel, bands), out_shape=(jax.Shape...]
    pallas_call x1, Pallas kernels: 43.6 us -> 43.1 us  [fast(): pl.pallas_call(functools.partial(fit_kernel, dates, bands, strips), out_s...]
where the time goes in v2:
time: 53 us; the launch traced here: 52.8 us
  Pallas kernels  52.1 us (98%)
  between operations  0.64 us (1%)
    pallas_call x1, Pallas kernels, fast(): pl.pallas_call(functools.partial(fit_kernel, dates, bands, strips), out_s...  43.1 us
    pallas_call x1, Pallas kernels, fast(): pl.pallas_call(functools.partial(lay_kernel, bands), out_shape=(jax.Shape...  9.09 us

profile of v2, /device:TPU:0, one launch (start us, length us, event | category | flops | bytes accessed | tf_op | source)
XLA Modules:
  0.0 52.8 jit_solution(2593086773571794083)
XLA Ops:
  0.6 43.1 %shard_map.76.recv = bf16[32,128,128]{2,1,0:T(8,128)(2,1)} custom-call(s32[2,60]{1,0:T(2,128)} %bitcast.2, s32[2,60]{1,0:T(2,128)} %bitcast.3, s32[60]{0:T(128)} %day_s.1, s32[2,1,256]{2,1,0:T(1,128)} %words.1, bf16[60,6,32,128]{3,2,1,0:T(8,128)(2,1)} %scenes.1), custom_call_target="tpu_custom_call" | custom-call | tf_op jit(solution)/shard_map/pallas_call | solution.py:540
  43.7 9.1 %shard_map.77 = (f32[8,6,4,1024]{3,2,1,0:T(4,128)}, f32[12,6,4,1024]{3,2,1,0:T(4,128)}, f32[6,4,1024]{2,1,0:T(4,128)}) custom-call(bf16[32,128,128]{2,1,0:T(8,128)(2,1)} %shard_map.76.recv), custom_call_target="tpu_custom_call" | custom-call | tf_op jit(solution)/shard_map/pallas_call | solution.py:566

commit v3 on v2

--- a/solution.py
+++ b/solution.py
@@ -445,7 +445,6 @@
                 return c2
 
             lax.fori_loop(0, half, push, 0)
-            lax.fori_loop(half + 1, strips, push, 0)
             return c
 
         done = jnp.where(s == bands - 1, groups, (21 * (s + 1)) // 16)
@@ -453,6 +452,15 @@
         return carry
 
     lax.fori_loop(0, bands, band, 0)
+
+    def push_near(k, c):
+        d = peer(k)
+        pltpu.make_async_remote_copy(
+            src_ref=send.at[d // 2, d % 2], dst_ref=out.at[me], send_sem=blk_send.at[d], recv_sem=blk_recv.at[me],
+            device_id={"band": d}, device_id_type=pl.DeviceIdType.MESH).start()
+        return c
+
+    lax.fori_loop(half + 1, strips, push_near, 0)
     own = pltpu.make_async_copy(send.at[me // 2, me % 2], out.at[me], own_sem.at[1])
     own.start()
 

time: 53 us -> 52.6 us (level)
  no operation moved by 1% of the time
where the time goes in v3:
time: 52.6 us; the launch traced here: 52.4 us
  Pallas kernels  51.8 us (98%)
  between operations  0.64 us (1%)
    pallas_call x1, Pallas kernels, fast(): pl.pallas_call(functools.partial(fit_kernel, dates, bands, strips), out_s...  42.7 us
    pallas_call x1, Pallas kernels, fast(): pl.pallas_call(functools.partial(lay_kernel, bands), out_shape=(jax.Shape...  9.09 us

profile of v3, /device:TPU:0, one launch (start us, length us, event | category | flops | bytes accessed | tf_op | source)
XLA Modules:
  0.0 52.4 jit_solution(5191107877511574760)
XLA Ops:
  0.6 42.7 %shard_map.76.recv = bf16[32,128,128]{2,1,0:T(8,128)(2,1)} custom-call(s32[2,60]{1,0:T(2,128)} %bitcast.2, s32[2,60]{1,0:T(2,128)} %bitcast.3, s32[60]{0:T(128)} %day_s.1, s32[2,1,256]{2,1,0:T(1,128)} %words.1, bf16[60,6,32,128]{3,2,1,0:T(8,128)(2,1)} %scenes.1), custom_call_target="tpu_custom_call" | custom-call | tf_op jit(solution)/shard_map/pallas_call | solution.py:548
  43.3 9.1 %shard_map.77 = (f32[8,6,4,1024]{3,2,1,0:T(4,128)}, f32[12,6,4,1024]{3,2,1,0:T(4,128)}, f32[6,4,1024]{2,1,0:T(4,128)}) custom-call(bf16[32,128,128]{2,1,0:T(8,128)(2,1)} %shard_map.76.recv), custom_call_target="tpu_custom_call" | custom-call | tf_op jit(solution)/shard_map/pallas_call | solution.py:574
